TPU v7x, 32 devices: a whole 2x2x4 slice. The times are simulated.
32 devices in a mesh: dp: 2 (over y), section: 4 (over z), mp: 4 (over x, core).
Axes of the slice: x: 2, y: 2, z: 4, core: 2. Of those that a mesh axis runs over, the one named last changes fastest.
Arguments:
- token_ids: int32 [32, 32], P('dp'), may hold values from 0 to 65535
- members: int32 [32], replicated, may hold values from 0 to 31, each once
- owners: int32 [4], replicated, may hold values from 0 to 3, each once
- embed_table: bfloat16 [4096, 65536], P('mp', 'section'), may hold values from -6 to 6
- norm_gain: float32 [4, 4096], P('section'), may hold values from 0.5 to 2
- gate_weight: bfloat16 [4, 4096, 10240], P('section', None, 'mp'), may hold values from -0.09375 to 0.09375
- up_weight: bfloat16 [4, 4096, 10240], P('section', None, 'mp'), may hold values from -0.09375 to 0.09375
- down_weight: bfloat16 [4, 4096, 10240], P('section', None, 'mp'), may hold values from -0.078125 to 0.078125
- final_gain: float32 [4096], replicated, may hold values from 0.5 to 2
- head_weight: bfloat16 [4096, 4096], P(None, 'mp'), may hold values from -0.0014648438 to 0.0014648438
Outputs:
- wins: float32 [4, 8, 8], P('dp', 'section')
Inputs may be any that keep to these rules, and one draw needn't show every extreme that they name: Prompt p's responses are members[8 * p] to members[8 * p + 7]; each response belongs to one prompt. `owners`: each slot holds one prompt.
All inputs are finite; a program needn't handle non-finite values.
Results may differ from a plain program's by a relative error of at most 0.028.
Values may be sent and summed in bfloat16 or wider, within the bound.
A program may use at most 192 MiB of HBM per device.

v0:
```python
import jax
import jax.numpy as jnp
from jax import lax
from jax.sharding import PartitionSpec as P

GROUP = 8
norm_eps = 1e-05
final_eps = 1e-06


def passed_along(value, axis, steps):
    count = lax.axis_size(axis)
    leading, last = (max(0, -steps), min(count, count - steps))
    return lax.ppermute(value, axis, [(source, source + steps) for source in range(leading, last)])


def broadcast(block, axis, source):
    block = jnp.where(lax.axis_index(axis) == source, block, jnp.zeros_like(block))
    return lax.psum(block, axis)


def contract_rows(weights, acts):
    return lax.dot_general(
        weights, acts, (((0,), (0,)), ((), ())), preferred_element_type=jnp.float32
    )


def activate(gate_acc, up_acc, squares, width):
    inverse = lax.rsqrt(squares / width + norm_eps)
    return (jax.nn.silu(gate_acc * inverse) * (up_acc * inverse)).astype(jnp.bfloat16)


def layer_split(state, gain, w_gate, w_up, w_down):
    width = gain.shape[0]
    wide = lax.all_gather(state, "mp", axis=0, tiled=True).astype(jnp.float32)
    scaled = (wide * gain[:, None]).astype(jnp.bfloat16)
    gate_acc = contract_rows(w_gate, scaled)
    up_acc = contract_rows(w_up, scaled)
    squares = jnp.sum(wide * wide, axis=0, keepdims=True)
    gate_acc, up_acc, squares = (gate_acc, up_acc, squares)
    hidden = activate(gate_acc, up_acc, squares, width)
    mixed = lax.psum_scatter(
        jnp.dot(w_down, hidden, preferred_element_type=jnp.float32).astype(jnp.bfloat16),
        "mp",
        scatter_dimension=0,
        tiled=True,
    ).astype(jnp.float32)
    return (state.astype(jnp.float32) + mixed).astype(jnp.bfloat16)


def per_device(
    token_ids,
    members,
    owners,
    embed_table,
    norm_gain,
    gate_weight,
    up_weight,
    down_weight,
    final_gain,
    head_weight,
):
    sections = lax.axis_size("section")
    section = lax.axis_index("section")
    vocab_part = embed_table.shape[1]
    flat = token_ids.reshape(-1)
    local_ids = flat - section * vocab_part
    inside = (local_ids >= 0) & (local_ids < vocab_part)
    picked = jnp.take(embed_table, jnp.clip(local_ids, 0, vocab_part - 1), axis=1)
    partial_value = jnp.where(inside[None, :], picked.astype(jnp.float32), 0.0)
    embedded = lax.psum(partial_value.astype(jnp.bfloat16), "section")
    gain = norm_gain[0]
    w_gate = gate_weight[0]
    w_up = up_weight[0]
    w_down = down_weight[0]
    block = embedded.shape[1] // sections
    state = jnp.zeros((embedded.shape[0], block), jnp.bfloat16)
    finished = []
    for tick in range(sections + sections - 1):
        if tick < sections:
            fresh = embedded[:, tick * block : (tick + 1) * block]
            state = jnp.where(section == 0, fresh, state)
        result = layer_split(state, gain, w_gate, w_up, w_down)
        if tick >= sections - 1:
            finished.append(result)
        if tick < sections + sections - 2:
            state = passed_along(result, "section", 1)
    final = jnp.concatenate(finished, axis=1)
    responses_here = token_ids.shape[0]
    length = token_ids.shape[1]
    pooled = jnp.mean(
        final.astype(jnp.float32).reshape(final.shape[0], responses_here, length), axis=2
    )
    groups_count = lax.axis_size("dp")
    parts = lax.axis_size("mp")
    stacked = lax.all_gather(pooled[None], ("dp", "mp"), axis=0, tiled=True)
    stacked = stacked.reshape(groups_count, parts, pooled.shape[0], responses_here)
    everyone = jnp.transpose(stacked, (1, 2, 0, 3)).reshape(
        parts * pooled.shape[0], groups_count * responses_here
    )
    factor = lax.rsqrt(jnp.mean(everyone * everyone, axis=0, keepdims=True) + final_eps)
    normed = (everyone * factor * final_gain[:, None]).astype(jnp.bfloat16)
    head_cols = head_weight.shape[1]
    projected = contract_rows(head_weight, normed)
    mine = lax.dynamic_slice_in_dim(normed, lax.axis_index("mp") * head_cols, head_cols).astype(
        jnp.float32
    )
    partial_scores = lax.dot_general(
        projected,
        mine,
        (((0,), (0,)), ((), ())),
        precision=lax.Precision.HIGHEST,
        preferred_element_type=jnp.float32,
    )
    scores = lax.psum(partial_scores, "mp")
    scores = broadcast(scores, "section", sections - 1)
    preference = jax.nn.sigmoid(scores - scores.T)
    prompt_count = owners.shape[0]
    local_prompts = prompt_count // lax.axis_size("dp")
    rows_local = GROUP // sections
    slot_here = lax.axis_index("dp") * local_prompts + jnp.arange(local_prompts, dtype=jnp.int32)
    match = (owners[None, :] == slot_here[:, None]).astype(jnp.int32)
    prompt_here = jnp.sum(match * jnp.arange(prompt_count, dtype=jnp.int32)[None, :], axis=1)
    groups = members.reshape(prompt_count, GROUP)
    chosen = groups[prompt_here]
    row_ids = lax.dynamic_slice_in_dim(chosen, section * rows_local, rows_local, 1)
    return preference[row_ids[:, :, None], chosen[:, None, :]]


def solution(mesh):
    placed = (
        P("dp", None),
        P(),
        P(),
        P("mp", "section"),
        P("section", None),
        P("section", None, "mp"),
        P("section", None, "mp"),
        P("section", None, "mp"),
        P(),
        P(None, "mp"),
    )
    return jax.shard_map(
        per_device, mesh=mesh, in_specs=placed, out_specs=P("dp", "section", None), check_vma=False
    )
```

profile of v0, /device:TPU:0, one launch (start us, length us, event | category | flops | bytes accessed | tf_op | source)
XLA Modules:
  0.0 752.2 jit_solution(12075295378497106360)
XLA Ops:
  8.2 43.9 %copy.26 = bf16[1024,16384]{0,1:T(8,128)(2,1)} copy(bf16[1024,16384]{1,0:T(8,128)(2,1)} %param.13) | data formatting | bytes 67108864 | tf_op args[3]
  52.1 16.3 %gather_fusion = bf16[512,1024]{1,0:T(8,128)(2,1)S(1)} fusion(bf16[1024,16384]{0,1:T(8,128)(2,1)} %copy.26, s32[1024]{0:T(1024)S(1)} %pad_clamp_fusion.1), kind=kCustom, calls=%fused_computation | custom fusion | bytes 2099200 | tf_op jit(solution)/shard_map/jit(_take)/gather | solution.py:69
  69.9 54.7 %all-reduce.2.cloned.1.call-done = bf16[1024,512]{0,1:T(8,128)(2,1)} async-done(((bf16[1024,512]{0,1:T(8,128)(2,1)}), bf16[1024,512]{0,1:T(8,128)(2,1)}) %all-reduce.2.cloned.1.call-update) | async-done | bytes 1048592 | tf_op jit(solution)/shard_map/psum | solution.py:71
  126.3 16.1 %all-gather.9.cloned.1.call-done = bf16[4096,128]{0,1:T(8,128)(2,1)} async-done(((bf16[1024,128]{0,1:T(8,128)(2,1)}), bf16[4096,128]{0,1:T(8,128)(2,1)}) %all-gather.9.cloned.1.call-update) | async-done | bytes 1048592 | tf_op jit(solution)/shard_map/all_gather | solution.py:35
  143.9 11.3 %fusion.87 = f32[2560,128]{0,1:T(8,128)} fusion(bf16[1,4096,2560]{2,1,0:T(8,128)(2,1)} %param.15, bf16[4096,128]{0,1:T(8,128)(2,1)} %all-gather.9.cloned.1.call-done, f32[4096]{0:T(1024)S(1)} %bitcast.292, f32[128]{0:T(128)S(1)} %add_rsqrt_fusion.7), kind=kOutput, calls=%fused_computation.60 | convolution fusion | flops 2686255104 | bytes 23347712 | tf_op jit(solution)/shard_map/dot_general | solution.py:23
  155.3 18.6 %fusion.81 = bf16[4096,128]{0,1:T(8,128)(2,1)} fusion(bf16[1,4096,2560]{2,1,0:T(8,128)(2,1)} %param.17, bf16[1,4096,2560]{2,1,0:T(8,128)(2,1)} %param.16, f32[2560,128]{0,1:T(8,128)} %fusion.87, bf16[4096,128]{0,1:T(8,128)(2,1)S(1)} %copy-done, f32[4096]{0:T(1024)S(1)} %bitcast.293, f32[128]{0:T(128)S(1)} %add_rsqrt_fusion.7), kind=kOutput, calls=%fused_computation.58 | convolution fusion | flops 5373100032 | bytes 45367808 | tf_op jit(solution)/shard_map/dot_general | solution.py:43
  173.9 24.9 %reduce-scatter.8.cloned.1.call-done = bf16[1024,128]{0,1:T(8,128)(2,1)} async-done(((bf16[4096,128]{0,1:T(8,128)(2,1)}), bf16[1024,128]{0,1:T(8,128)(2,1)}) %reduce-scatter.8.cloned.1.call-update) | async-done | bytes 262160 | tf_op jit(solution)/shard_map/reduce_scatter | solution.py:42
  210.0 17.3 %all-gather.11.cloned.1.call-done = bf16[4096,128]{0,1:T(8,128)(2,1)} async-done(((bf16[1024,128]{0,1:T(8,128)(2,1)}), bf16[4096,128]{0,1:T(8,128)(2,1)}) %all-gather.11.cloned.1.call-update) | async-done | bytes 1048592 | tf_op jit(solution)/shard_map/all_gather | solution.py:35
  228.8 11.3 %fusion.93 = f32[2560,128]{0,1:T(8,128)} fusion(bf16[1,4096,2560]{2,1,0:T(8,128)(2,1)} %param.15, bf16[4096,128]{0,1:T(8,128)(2,1)} %all-gather.11.cloned.1.call-done, f32[4096]{0:T(1024)S(1)} %bitcast.294, f32[128]{0:T(128)S(1)} %add_rsqrt_fusion.6), kind=kOutput, calls=%fused_computation.62 | convolution fusion | flops 2686255104 | bytes 23347712 | tf_op jit(solution)/shard_map/dot_general | solution.py:23
  240.1 18.5 %fusion.78 = bf16[4096,128]{0,1:T(8,128)(2,1)} fusion(bf16[1,4096,2560]{2,1,0:T(8,128)(2,1)} %param.17, bf16[1,4096,2560]{2,1,0:T(8,128)(2,1)} %param.16, f32[2560,128]{0,1:T(8,128)} %fusion.93, bf16[4096,128]{0,1:T(8,128)(2,1)S(1)} %copy-done.1, f32[4096]{0:T(1024)S(1)} %bitcast.295, f32[128]{0:T(128)S(1)} %add_rsqrt_fusion.6), kind=kOutput, calls=%fused_computation.57 | convolution fusion | flops 5373100032 | bytes 45367808 | tf_op jit(solution)/shard_map/dot_general | solution.py:43
  258.7 24.9 %reduce-scatter.10.cloned.1.call-done = bf16[1024,128]{0,1:T(8,128)(2,1)} async-done(((bf16[4096,128]{0,1:T(8,128)(2,1)}), bf16[1024,128]{0,1:T(8,128)(2,1)}) %reduce-scatter.10.cloned.1.call-update) | async-done | bytes 262160 | tf_op jit(solution)/shard_map/reduce_scatter | solution.py:42
  294.2 17.8 %all-gather.13.cloned.1.call-done = bf16[4096,128]{0,1:T(8,128)(2,1)} async-done(((bf16[1024,128]{0,1:T(8,128)(2,1)}), bf16[4096,128]{0,1:T(8,128)(2,1)}) %all-gather.13.cloned.1.call-update) | async-done | bytes 1048592 | tf_op jit(solution)/shard_map/all_gather | solution.py:35
  313.6 11.3 %fusion.99 = f32[2560,128]{0,1:T(8,128)} fusion(bf16[1,4096,2560]{2,1,0:T(8,128)(2,1)} %param.15, bf16[4096,128]{0,1:T(8,128)(2,1)} %all-gather.13.cloned.1.call-done, f32[4096]{0:T(1024)S(1)} %bitcast.296, f32[128]{0:T(128)S(1)} %add_rsqrt_fusion.5), kind=kOutput, calls=%fused_computation.64 | convolution fusion | flops 2686255104 | bytes 23347712 | tf_op jit(solution)/shard_map/dot_general | solution.py:23
  324.9 18.5 %fusion.75 = bf16[4096,128]{0,1:T(8,128)(2,1)} fusion(bf16[1,4096,2560]{2,1,0:T(8,128)(2,1)} %param.17, bf16[1,4096,2560]{2,1,0:T(8,128)(2,1)} %param.16, f32[2560,128]{0,1:T(8,128)} %fusion.99, bf16[4096,128]{0,1:T(8,128)(2,1)S(1)} %copy-done.2, f32[4096]{0:T(1024)S(1)} %bitcast.297, f32[128]{0:T(128)S(1)} %add_rsqrt_fusion.5), kind=kOutput, calls=%fused_computation.56 | convolution fusion | flops 5373100032 | bytes 45367808 | tf_op jit(solution)/shard_map/dot_general | solution.py:43
  343.7 24.7 %reduce-scatter.12.cloned.1.call-done = bf16[1024,128]{0,1:T(8,128)(2,1)} async-done(((bf16[4096,128]{0,1:T(8,128)(2,1)}), bf16[1024,128]{0,1:T(8,128)(2,1)}) %reduce-scatter.12.cloned.1.call-update) | async-done | bytes 262160 | tf_op jit(solution)/shard_map/reduce_scatter | solution.py:42
  379.0 17.8 %all-gather.15.cloned.1.call-done = bf16[4096,128]{0,1:T(8,128)(2,1)} async-done(((bf16[1024,128]{0,1:T(8,128)(2,1)}), bf16[4096,128]{0,1:T(8,128)(2,1)}) %all-gather.15.cloned.1.call-update) | async-done | bytes 1048592 | tf_op jit(solution)/shard_map/all_gather | solution.py:35
  407.3 18.3 %fusion.72 = bf16[4096,128]{0,1:T(8,128)(2,1)} fusion(bf16[1,4096,2560]{2,1,0:T(8,128)(2,1)} %param.17, bf16[1,4096,2560]{2,1,0:T(8,128)(2,1)} %param.16, f32[2560,128]{0,1:T(8,128)S(1)} %fusion.105, bf16[4096,128]{0,1:T(8,128)(2,1)S(1)} %copy-done.3, f32[4096]{0:T(1024)S(1)} %bitcast.299, f32[128]{0:T(128)S(1)} %add_rsqrt_fusion.4), kind=kOutput, calls=%fused_computation.55 | convolution fusion | flops 5373100032 | bytes 45367808 | tf_op jit(solution)/shard_map/dot_general | solution.py:43
  425.7 24.9 %reduce-scatter.14.cloned.1.call-done = bf16[1024,128]{0,1:T(8,128)(2,1)} async-done(((bf16[4096,128]{0,1:T(8,128)(2,1)}), bf16[1024,128]{0,1:T(8,128)(2,1)}) %reduce-scatter.14.cloned.1.call-update) | async-done | bytes 262160 | tf_op jit(solution)/shard_map/reduce_scatter | solution.py:42
  461.1 17.8 %all-gather.17.cloned.1.call-done = bf16[4096,128]{0,1:T(8,128)(2,1)} async-done(((bf16[1024,128]{0,1:T(8,128)(2,1)}), bf16[4096,128]{0,1:T(8,128)(2,1)}) %all-gather.17.cloned.1.call-update) | async-done | bytes 1048592 | tf_op jit(solution)/shard_map/all_gather | solution.py:35
  489.4 18.3 %fusion.69 = bf16[4096,128]{0,1:T(8,128)(2,1)} fusion(bf16[1,4096,2560]{2,1,0:T(8,128)(2,1)} %param.17, bf16[1,4096,2560]{2,1,0:T(8,128)(2,1)} %param.16, f32[2560,128]{0,1:T(8,128)S(1)} %fusion.111, bf16[4096,128]{0,1:T(8,128)(2,1)S(1)} %copy-done.4, f32[4096]{0:T(1024)S(1)} %bitcast.301, f32[128]{0:T(128)S(1)} %add_rsqrt_fusion.3), kind=kOutput, calls=%fused_computation.54 | convolution fusion | flops 5373100032 | bytes 45367808 | tf_op jit(solution)/shard_map/dot_general | solution.py:43
  507.8 24.9 %reduce-scatter.16.cloned.1.call-done = bf16[1024,128]{0,1:T(8,128)(2,1)} async-done(((bf16[4096,128]{0,1:T(8,128)(2,1)}), bf16[1024,128]{0,1:T(8,128)(2,1)}) %reduce-scatter.16.cloned.1.call-update) | async-done | bytes 262160 | tf_op jit(solution)/shard_map/reduce_scatter | solution.py:42
  543.5 17.6 %all-gather.19.cloned.1.call-done = bf16[4096,128]{0,1:T(8,128)(2,1)} async-done(((bf16[1024,128]{0,1:T(8,128)(2,1)}), bf16[4096,128]{0,1:T(8,128)(2,1)}) %all-gather.19.cloned.1.call-update) | async-done | bytes 1048592 | tf_op jit(solution)/shard_map/all_gather | solution.py:35
  562.6 8.9 %fusion.117 = f32[2560,128]{0,1:T(8,128)S(1)} fusion(bf16[1,4096,2560]{2,1,0:T(8,128)(2,1)} %param.15, bf16[4096,128]{0,1:T(8,128)(2,1)} %all-gather.19.cloned.1.call-done, f32[4096]{0:T(1024)S(1)} %bitcast.302, f32[128]{0:T(128)S(1)} %add_rsqrt_fusion.2), kind=kOutput, calls=%fused_computation.70 | convolution fusion | flops 2686255104 | bytes 23347712 | tf_op jit(solution)/shard_map/dot_general | solution.py:23
  571.6 18.3 %fusion.66 = bf16[4096,128]{0,1:T(8,128)(2,1)} fusion(bf16[1,4096,2560]{2,1,0:T(8,128)(2,1)} %param.17, bf16[1,4096,2560]{2,1,0:T(8,128)(2,1)} %param.16, f32[2560,128]{0,1:T(8,128)S(1)} %fusion.117, bf16[4096,128]{0,1:T(8,128)(2,1)S(1)} %copy-done.5, f32[4096]{0:T(1024)S(1)} %bitcast.303, f32[128]{0:T(128)S(1)} %add_rsqrt_fusion.2), kind=kOutput, calls=%fused_computation.53 | convolution fusion | flops 5373100032 | bytes 45367808 | tf_op jit(solution)/shard_map/dot_general | solution.py:43
  589.9 24.9 %reduce-scatter.18.cloned.1.call-done = bf16[1024,128]{0,1:T(8,128)(2,1)} async-done(((bf16[4096,128]{0,1:T(8,128)(2,1)}), bf16[1024,128]{0,1:T(8,128)(2,1)}) %reduce-scatter.18.cloned.1.call-update) | async-done | bytes 262160 | tf_op jit(solution)/shard_map/reduce_scatter | solution.py:42
  625.4 17.8 %all-gather.21.cloned.1.call-done = bf16[4096,128]{0,1:T(8,128)(2,1)} async-done(((bf16[1024,128]{0,1:T(8,128)(2,1)}), bf16[4096,128]{0,1:T(8,128)(2,1)}) %all-gather.21.cloned.1.call-update) | async-done | bytes 1048592 | tf_op jit(solution)/shard_map/all_gather | solution.py:35
  644.8 8.9 %fusion.123 = f32[2560,128]{0,1:T(8,128)S(1)} fusion(bf16[1,4096,2560]{2,1,0:T(8,128)(2,1)} %param.15, bf16[4096,128]{0,1:T(8,128)(2,1)} %all-gather.21.cloned.1.call-done, f32[4096]{0:T(1024)S(1)} %bitcast.304, f32[128]{0:T(128)S(1)} %add_rsqrt_fusion.1), kind=kOutput, calls=%fused_computation.72 | convolution fusion | flops 2686255104 | bytes 23347712 | tf_op jit(solution)/shard_map/dot_general | solution.py:23
  653.7 18.3 %fusion.63 = bf16[4096,128]{0,1:T(8,128)(2,1)} fusion(bf16[1,4096,2560]{2,1,0:T(8,128)(2,1)} %param.17, bf16[1,4096,2560]{2,1,0:T(8,128)(2,1)} %param.16, f32[2560,128]{0,1:T(8,128)S(1)} %fusion.123, bf16[4096,128]{0,1:T(8,128)(2,1)S(1)} %copy-done.6, f32[4096]{0:T(1024)S(1)} %bitcast.305, f32[128]{0:T(128)S(1)} %add_rsqrt_fusion.1), kind=kOutput, calls=%fused_computation.52 | convolution fusion | flops 5373100032 | bytes 45367808 | tf_op jit(solution)/shard_map/dot_general | solution.py:43
  673.1 23.8 %reduce-scatter.20.cloned.1.call-done = bf16[1024,128]{0,1:T(8,128)(2,1)} async-done(((bf16[4096,128]{0,1:T(8,128)(2,1)}), bf16[1024,128]{0,1:T(8,128)(2,1)}) %reduce-scatter.20.cloned.1.call-update) | async-done | bytes 262160 | tf_op jit(solution)/shard_map/reduce_scatter | solution.py:42
  698.3 10.1 %all-gather = f32[8192,16]{0,1:T(8,128)S(1)} all-gather(f32[1024,16]{0,1:T(8,128)S(1)} %broadcast_multiply_fusion), channel_id=2, replica_groups=mesh['dp'=2,'section'=4,'mp'=4] {'dp','mp'}, dimensions={0}, use_global_device_ids=true | all-gather | bytes 589824 | tf_op jit(solution)/shard_map/all_gather | solution.py:96
  714.7 10.5 %psum.22 = f32[32,32]{1,0:T(8,128)S(1)} all-reduce(f32[32,32]{1,0:T(8,128)S(1)} %fusion.309), channel_id=1, replica_groups=mesh['dp'=2,'section'=4,'mp'=4] {'mp'}, use_global_device_ids=true, to_apply=%region_17.18 | all-reduce | flops 1024 | bytes 8192 | tf_op jit(solution)/shard_map/psum | solution.py:115
  725.2 18.7 %psum.23 = f32[32,32]{1,0:T(8,128)S(1)} all-reduce(f32[32,32]{1,0:T(8,128)S(1)} %broadcast_select_fusion), channel_id=1, replica_groups=mesh['dp'=2,'section'=4,'mp'=4] {'section'}, use_global_device_ids=true, to_apply=%region_18.19 | all-reduce | flops 1024 | bytes 8192 | tf_op jit(solution)/shard_map/psum | solution.py:19
  (147 shorter events, 108.2 us)
Async XLA Ops:
  6.5 118.0 %all-reduce.2.cloned.1.call-start = ((), (), s32[]{:S(2)}) async-start(), calls=%async_computation.7 | async-start | bytes 2097152 | tf_op jit(solution)/shard_map/psum | solution.py:71
  68.5 75.4 %copy-start.7 = (f32[1,4096]{1,0:T(1,128)S(1)}, f32[1,4096]{1,0:T(1,128)}, u32[]{:S(2)}) copy-start(f32[1,4096]{1,0:T(1,128)} %param.14) | copy-start | bytes 49156
  69.8 72.6 %all-gather.9.cloned.1.call-start = ((), (), s32[]{:S(2)}) async-start(), calls=%async_computation.8 | async-start | bytes 1310720 | tf_op jit(solution)/shard_map/all_gather | solution.py:35
  126.3 72.6 %reduce-scatter.8.cloned.1.call-start = ((), (), s32[]{:S(2)}) async-start(), calls=%async_computation.9 | async-start | bytes 1310720 | tf_op jit(solution)/shard_map/reduce_scatter | solution.py:42
  155.3 43.5 %copy-start.11 = (bf16[1024,512]{0,1:T(8,128)(2,1)S(1)}, bf16[1024,512]{0,1:T(8,128)(2,1)}, u32[]{:S(2)}) copy-start(bf16[1024,512]{0,1:T(8,128)(2,1)} %all-reduce.2.cloned.1.call-done) | copy-start | bytes 3145732
  173.9 53.4 %all-gather.11.cloned.1.call-start = ((), (), s32[]{:S(2)}) async-start(), calls=%async_computation.10 | async-start | bytes 1310720 | tf_op jit(solution)/shard_map/all_gather | solution.py:35
  199.9 8.8 %collective-permute-start = (bf16[1024,128]{0,1:T(8,128)(2,1)S(1)}, bf16[1024,128]{0,1:T(8,128)(2,1)S(1)}, u32[]{:S(2)}, u32[]{:S(2)}) collective-permute-start(bf16[1024,128]{0,1:T(8,128)(2,1)S(1)} %add_convert_fusion.6), channel_id=1, source_target_pairs={{0,4},{4,8},{8,12},{1,5},{5,9},{9,13},{2,6},{6,10},{10,14},{3,7},{... | collective-permute-start | bytes 786440 | tf_op jit(solution)/shard_map/ppermute | solution.py:14
  209.4 74.2 %reduce-scatter.10.cloned.1.call-start = ((), (), s32[]{:S(2)}) async-start(), calls=%async_computation.11 | async-start | bytes 1310720 | tf_op jit(solution)/shard_map/reduce_scatter | solution.py:42
  240.1 43.5 %copy-start.9 = (bf16[1024,128]{0,1:T(8,128)(2,1)S(1)}, bf16[1024,128]{0,1:T(8,128)(2,1)}, u32[]{:S(2)}) copy-start(bf16[1024,128]{0,1:T(8,128)(2,1)} %slice_select_fusion.1) | copy-start | bytes 786436
  258.6 53.4 %all-gather.13.cloned.1.call-start = ((), (), s32[]{:S(2)}) async-start(), calls=%async_computation.12 | async-start | bytes 1310720 | tf_op jit(solution)/shard_map/all_gather | solution.py:35
  284.6 8.8 %collective-permute-start.1 = (bf16[1024,128]{0,1:T(8,128)(2,1)S(1)}, bf16[1024,128]{0,1:T(8,128)(2,1)S(1)}, u32[]{:S(2)}, u32[]{:S(2)}) collective-permute-start(bf16[1024,128]{0,1:T(8,128)(2,1)S(1)} %add_convert_fusion.5), channel_id=1, source_target_pairs={{0,4},{4,8},{8,12},{1,5},{5,9},{9,13},{2,6},{6,10},{10,14},{3,7},{... | collective-permute-start | bytes 786440 | tf_op jit(solution)/shard_map/ppermute | solution.py:14
  294.2 74.2 %reduce-scatter.12.cloned.1.call-start = ((), (), s32[]{:S(2)}) async-start(), calls=%async_computation.13 | async-start | bytes 1310720 | tf_op jit(solution)/shard_map/reduce_scatter | solution.py:42
  313.6 11.4 %copy-start.2 = (bf16[4096,128]{0,1:T(8,128)(2,1)S(1)}, bf16[4096,128]{0,1:T(8,128)(2,1)}, u32[]{:S(2)}) copy-start(bf16[4096,128]{0,1:T(8,128)(2,1)} %all-gather.13.cloned.1.call-done) | copy-start | bytes 3145732
  324.9 43.5 %copy-start.10 = (bf16[1024,128]{0,1:T(8,128)(2,1)S(1)}, bf16[1024,128]{0,1:T(8,128)(2,1)}, u32[]{:S(2)}) copy-start(bf16[1024,128]{0,1:T(8,128)(2,1)} %slice_select_fusion.2) | copy-start | bytes 786436
  343.4 53.4 %all-gather.15.cloned.1.call-start = ((), (), s32[]{:S(2)}) async-start(), calls=%async_computation.14 | async-start | bytes 1310720 | tf_op jit(solution)/shard_map/all_gather | solution.py:35
  369.4 8.8 %collective-permute-start.2 = (bf16[1024,128]{0,1:T(8,128)(2,1)S(1)}, bf16[1024,128]{0,1:T(8,128)(2,1)S(1)}, u32[]{:S(2)}, u32[]{:S(2)}) collective-permute-start(bf16[1024,128]{0,1:T(8,128)(2,1)S(1)} %add_convert_fusion.4), channel_id=1, source_target_pairs={{0,4},{4,8},{8,12},{1,5},{5,9},{9,13},{2,6},{6,10},{10,14},{3,7},{... | collective-permute-start | bytes 786440 | tf_op jit(solution)/shard_map/ppermute | solution.py:14
  378.9 71.6 %reduce-scatter.14.cloned.1.call-start = ((), (), s32[]{:S(2)}) async-start(), calls=%async_computation.15 | async-start | bytes 1310720 | tf_op jit(solution)/shard_map/reduce_scatter | solution.py:42
  407.3 43.3 %copy-start.8 = (bf16[1024,128]{0,1:T(8,128)(2,1)S(1)}, bf16[1024,128]{0,1:T(8,128)(2,1)}, u32[]{:S(2)}) copy-start(bf16[1024,128]{0,1:T(8,128)(2,1)} %slice_select_fusion.3) | copy-start | bytes 786436
  425.6 53.3 %all-gather.17.cloned.1.call-start = ((), (), s32[]{:S(2)}) async-start(), calls=%async_computation.16 | async-start | bytes 1310720 | tf_op jit(solution)/shard_map/all_gather | solution.py:35
  451.6 8.8 %collective-permute-start.3 = (bf16[1024,128]{0,1:T(8,128)(2,1)S(1)}, bf16[1024,128]{0,1:T(8,128)(2,1)S(1)}, u32[]{:S(2)}, u32[]{:S(2)}) collective-permute-start(bf16[1024,128]{0,1:T(8,128)(2,1)S(1)} %add_convert_fusion.3), channel_id=1, source_target_pairs={{0,4},{4,8},{8,12},{1,5},{5,9},{9,13},{2,6},{6,10},{10,14},{3,7},{... | collective-permute-start | bytes 786440 | tf_op jit(solution)/shard_map/ppermute | solution.py:14
  461.1 71.6 %reduce-scatter.16.cloned.1.call-start = ((), (), s32[]{:S(2)}) async-start(), calls=%async_computation.17 | async-start | bytes 1310720 | tf_op jit(solution)/shard_map/reduce_scatter | solution.py:42
  489.4 43.3 %copy-start.15 = (bf16[1024,128]{0,1:T(8,128)(2,1)S(1)}, bf16[1024,128]{0,1:T(8,128)(2,1)}, u32[]{:S(2)}) copy-start(bf16[1024,128]{0,1:T(8,128)(2,1)} %copy-done.14) | copy-start | bytes 786436
  507.7 53.4 %all-gather.19.cloned.1.call-start = ((), (), s32[]{:S(2)}) async-start(), calls=%async_computation.18 | async-start | bytes 1310720 | tf_op jit(solution)/shard_map/all_gather | solution.py:35
  533.7 8.8 %collective-permute-start.4 = (bf16[1024,128]{0,1:T(8,128)(2,1)S(1)}, bf16[1024,128]{0,1:T(8,128)(2,1)S(1)}, u32[]{:S(2)}, u32[]{:S(2)}) collective-permute-start(bf16[1024,128]{0,1:T(8,128)(2,1)S(1)} %add_convert_fusion.2), channel_id=1, source_target_pairs={{0,4},{4,8},{8,12},{1,5},{5,9},{9,13},{2,6},{6,10},{10,14},{3,7},{... | collective-permute-start | bytes 786440 | tf_op jit(solution)/shard_map/ppermute | solution.py:14
  543.2 71.6 %reduce-scatter.18.cloned.1.call-start = ((), (), s32[]{:S(2)}) async-start(), calls=%async_computation.19 | async-start | bytes 1310720 | tf_op jit(solution)/shard_map/reduce_scatter | solution.py:42
  571.6 43.2 %copy-start.17 = (bf16[1024,128]{0,1:T(8,128)(2,1)S(1)}, bf16[1024,128]{0,1:T(8,128)(2,1)}, u32[]{:S(2)}) copy-start(bf16[1024,128]{0,1:T(8,128)(2,1)} %copy-done.16) | copy-start | bytes 786436
  589.9 53.3 %all-gather.21.cloned.1.call-start = ((), (), s32[]{:S(2)}) async-start(), calls=%async_computation.20 | async-start | bytes 1310720 | tf_op jit(solution)/shard_map/all_gather | solution.py:35
  615.8 8.8 %collective-permute-start.5 = (bf16[1024,128]{0,1:T(8,128)(2,1)S(1)}, bf16[1024,128]{0,1:T(8,128)(2,1)S(1)}, u32[]{:S(2)}, u32[]{:S(2)}) collective-permute-start(bf16[1024,128]{0,1:T(8,128)(2,1)S(1)} %add_convert_fusion.1), channel_id=1, source_target_pairs={{0,4},{4,8},{8,12},{1,5},{5,9},{9,13},{2,6},{6,10},{10,14},{3,7},{... | collective-permute-start | bytes 786440 | tf_op jit(solution)/shard_map/ppermute | solution.py:14
  625.4 71.6 %reduce-scatter.20.cloned.1.call-start = ((), (), s32[]{:S(2)}) async-start(), calls=%async_computation.21 | async-start | bytes 1310720 | tf_op jit(solution)/shard_map/reduce_scatter | solution.py:42
  653.7 18.4 %copy-start.19 = (s32[32]{0:T(128)S(1)}, s32[32]{0:T(128)}, u32[]{:S(2)}) copy-start(s32[32]{0:T(128)} %param.11) | copy-start | bytes 388
  653.7 18.4 %copy-start.20 = (s32[4]{0:T(128)S(1)}, s32[4]{0:T(128)}, u32[]{:S(2)}) copy-start(s32[4]{0:T(128)} %param.12) | copy-start | bytes 52
  653.7 43.3 %copy-start.13 = (bf16[1024,128]{0,1:T(8,128)(2,1)S(1)}, bf16[1024,128]{0,1:T(8,128)(2,1)}, u32[]{:S(2)}) copy-start(bf16[1024,128]{0,1:T(8,128)(2,1)} %copy-done.12) | copy-start | bytes 786436
  (10 other events, 71.8 us)
Sparse Core Ops, SparseCore 0:
  69.9 54.5 all-reduce.1
  126.4 15.9 all-gather.8
  174.0 24.7 reduce-scatter.7
  209.5 17.6 all-gather.10
  258.8 24.8 reduce-scatter.9
  294.3 17.6 all-gather.12
  343.6 24.7 reduce-scatter.11
  379.1 17.7 all-gather.14
  425.7 24.7 reduce-scatter.13
  461.2 17.6 all-gather.16
  507.9 24.7 reduce-scatter.15
  543.3 17.7 all-gather.18
  590.0 24.7 reduce-scatter.17
  625.5 17.6 all-gather.20
  672.1 24.7 reduce-scatter.19
where the time goes:
time: 761 us; the launch traced here: 752 us
  waiting for transfers between devices  382 us (50%)
  matrix products  204 us (27%)
  local copies, waits for them, and re-layouts  65.8 us (9%)
  blocking collectives  39.3 us (5%)
  other arithmetic  25.4 us (3%)
  starting transfers between devices  21.9 us (3%)
  between operations  14 us (2%)
    reduce_scatter x7, waiting for transfers between devices, layer_split(): lax.psum_scatter(jnp.dot(w_down, hidden, preferred_element_type=jnp.float...  173 us
    dot_general x7, matrix products, layer_split(): jnp.dot(w_down, hidden, preferred_element_type=jnp.float32)  129 us
    all_gather x7, waiting for transfers between devices, layer_split(): wide = lax.all_gather(state, 'mp', axis=0, tiled=True).astype(jnp.float32)  122 us
    dot_general x8, matrix products, contract_rows(): lax.dot_general(weights, acts, (((0,), (0,)), ((), ())), preferred_elemen...  74.6 us
    psum x1, waiting for transfers between devices, per_device(): embedded = lax.psum(partial_value.astype(jnp.bfloat16), 'section')  54.7 us
    unnamed x45, local copies, waits for them, and re-layouts  46.6 us
    ppermute x6, waiting for transfers between devices, passed_along(): lax.ppermute(value, axis, [(source, source + steps) for source in range(l...  32.2 us
    ppermute x6, starting transfers between devices, passed_along(): lax.ppermute(value, axis, [(source, source + steps) for source in range(l...  20.4 us
  transfers between devices with their start and end apart: 21, of which 21 were waited for; matrix products, arithmetic and copies ran while one was open for 0% of the time, Pallas kernels for 0%

commit v1 on v0

--- a/solution.py
+++ b/solution.py
@@ -68,7 +68,7 @@
     inside = (local_ids >= 0) & (local_ids < vocab_part)
     picked = jnp.take(embed_table, jnp.clip(local_ids, 0, vocab_part - 1), axis=1)
     partial_value = jnp.where(inside[None, :], picked.astype(jnp.float32), 0.0)
-    embedded = lax.psum(partial_value.astype(jnp.bfloat16), "section")
+    embedded = jnp.sum(lax.all_gather(partial_value.astype(jnp.bfloat16), "section"), axis=0)
     gain = norm_gain[0]
     w_gate = gate_weight[0]
     w_up = up_weight[0]

time: 761 us -> 785 us (1.032)
  waiting for transfers between devices: 382 us -> 410 us
  matrix products: 204 us -> 196 us
    all_gather x0 -> x1, waiting for transfers between devices: none -> 83.5 us  [per_device(): lax.all_gather(partial_value.astype(jnp.bfloat16), 'section')]
    psum x1 -> x0, waiting for transfers between devices: 54.7 us -> none  [per_device(): embedded = lax.psum(partial_value.astype(jnp.bfloat16), 'section')]
    unnamed x45 -> x47, local copies, waits for them, and re-layouts: 46.6 us -> 47.1 us
where the time goes in v1:
time: 785 us; the launch traced here: 776 us
  waiting for transfers between devices  410 us (52%)
  matrix products  196 us (25%)
  local copies, waits for them, and re-layouts  67.9 us (9%)
  blocking collectives  39.3 us (5%)
  other arithmetic  27 us (3%)
  starting transfers between devices  22 us (3%)
  between operations  14.1 us (2%)
    reduce_scatter x7, waiting for transfers between devices, layer_split(): lax.psum_scatter(jnp.dot(w_down, hidden, preferred_element_type=jnp.float...  173 us
    dot_general x7, matrix products, layer_split(): jnp.dot(w_down, hidden, preferred_element_type=jnp.float32)  128 us
    all_gather x7, waiting for transfers between devices, layer_split(): wide = lax.all_gather(state, 'mp', axis=0, tiled=True).astype(jnp.float32)  121 us
    all_gather x1, waiting for transfers between devices, per_device(): lax.all_gather(partial_value.astype(jnp.bfloat16), 'section')  83.5 us
    dot_general x8, matrix products, contract_rows(): lax.dot_general(weights, acts, (((0,), (0,)), ((), ())), preferred_elemen...  67.4 us
    unnamed x47, local copies, waits for them, and re-layouts  47.1 us
    ppermute x6, waiting for transfers between devices, passed_along(): lax.ppermute(value, axis, [(source, source + steps) for source in range(l...  31.7 us
    ppermute x6, starting transfers between devices, passed_along(): lax.ppermute(value, axis, [(source, source + steps) for source in range(l...  20.5 us
  transfers between devices with their start and end apart: 21, of which 21 were waited for; matrix products, arithmetic and copies ran while one was open for 0% of the time, Pallas kernels for 0%

profile of v1, /device:TPU:0, one launch (start us, length us, event | category | flops | bytes accessed | tf_op | source)
XLA Modules:
  0.0 775.8 jit_solution(7889346779997077806)
XLA Ops:
  8.2 43.9 %copy.41 = bf16[1024,16384]{0,1:T(8,128)(2,1)} copy(bf16[1024,16384]{1,0:T(8,128)(2,1)} %param.13) | data formatting | bytes 67108864 | tf_op args[3]
  52.1 16.3 %gather_fusion = bf16[512,1024]{1,0:T(8,128)(2,1)S(1)} fusion(bf16[1024,16384]{0,1:T(8,128)(2,1)} %copy.41, s32[1024]{0:T(1024)S(1)} %pad_clamp_fusion.1), kind=kCustom, calls=%fused_computation | custom fusion | bytes 2099200 | tf_op jit(solution)/shard_map/jit(_take)/gather | solution.py:69
  70.2 83.5 %all-gather.10.cloned.1.call-done = bf16[4,1024,512]{2,1,0:T(8,128)(2,1)} async-done(((bf16[1,1024,512]{2,1,0:T(8,128)(2,1)}), bf16[4,1024,512]{2,1,0:T(8,128)(2,1)}) %all-gather.10.cloned.1.call-update) | async-done | bytes 4194320 | tf_op jit(solution)/shard_map/all_gather | solution.py:71
  158.4 15.3 %all-gather.12.cloned.1.call-done = bf16[4096,128]{0,1:T(8,128)(2,1)} async-done(((bf16[1024,128]{0,1:T(8,128)(2,1)}), bf16[4096,128]{0,1:T(8,128)(2,1)}) %all-gather.12.cloned.1.call-update) | async-done | bytes 1048592 | tf_op jit(solution)/shard_map/all_gather | solution.py:35
  184.2 18.3 %fusion.81 = bf16[4096,128]{0,1:T(8,128)(2,1)} fusion(bf16[1,4096,2560]{2,1,0:T(8,128)(2,1)} %param.17, bf16[1,4096,2560]{2,1,0:T(8,128)(2,1)} %param.16, f32[2560,128]{0,1:T(8,128)S(1)} %fusion.87, bf16[4096,128]{0,1:T(8,128)(2,1)S(1)} %copy-done, f32[4096]{0:T(1024)S(1)} %bitcast.297, f32[128]{0:T(128)S(1)} %add_rsqrt_fusion.7), kind=kOutput, calls=%fused_computation.58 | convolution fusion | flops 5373100032 | bytes 45367808 | tf_op jit(solution)/shard_map/dot_general | solution.py:43
  202.6 24.9 %reduce-scatter.8.cloned.1.call-done = bf16[1024,128]{0,1:T(8,128)(2,1)} async-done(((bf16[4096,128]{0,1:T(8,128)(2,1)}), bf16[1024,128]{0,1:T(8,128)(2,1)}) %reduce-scatter.8.cloned.1.call-update) | async-done | bytes 262160 | tf_op jit(solution)/shard_map/reduce_scatter | solution.py:42
  238.6 17.3 %all-gather.14.cloned.1.call-done = bf16[4096,128]{0,1:T(8,128)(2,1)} async-done(((bf16[1024,128]{0,1:T(8,128)(2,1)}), bf16[4096,128]{0,1:T(8,128)(2,1)}) %all-gather.14.cloned.1.call-update) | async-done | bytes 1048592 | tf_op jit(solution)/shard_map/all_gather | solution.py:35
  257.4 8.9 %fusion.93 = f32[2560,128]{0,1:T(8,128)S(1)} fusion(bf16[1,4096,2560]{2,1,0:T(8,128)(2,1)} %param.15, bf16[4096,128]{0,1:T(8,128)(2,1)} %all-gather.14.cloned.1.call-done, f32[4096]{0:T(1024)S(1)} %bitcast.298, f32[128]{0:T(128)S(1)} %add_rsqrt_fusion.6), kind=kOutput, calls=%fused_computation.62 | convolution fusion | flops 2686255104 | bytes 23347712 | tf_op jit(solution)/shard_map/dot_general | solution.py:23
  266.4 18.3 %fusion.78 = bf16[4096,128]{0,1:T(8,128)(2,1)} fusion(bf16[1,4096,2560]{2,1,0:T(8,128)(2,1)} %param.17, bf16[1,4096,2560]{2,1,0:T(8,128)(2,1)} %param.16, f32[2560,128]{0,1:T(8,128)S(1)} %fusion.93, bf16[4096,128]{0,1:T(8,128)(2,1)S(1)} %copy-done.1, f32[4096]{0:T(1024)S(1)} %bitcast.299, f32[128]{0:T(128)S(1)} %add_rsqrt_fusion.6), kind=kOutput, calls=%fused_computation.57 | convolution fusion | flops 5373100032 | bytes 45367808 | tf_op jit(solution)/shard_map/dot_general | solution.py:43
  284.7 24.9 %reduce-scatter.10.cloned.1.call-done = bf16[1024,128]{0,1:T(8,128)(2,1)} async-done(((bf16[4096,128]{0,1:T(8,128)(2,1)}), bf16[1024,128]{0,1:T(8,128)(2,1)}) %reduce-scatter.10.cloned.1.call-update) | async-done | bytes 262160 | tf_op jit(solution)/shard_map/reduce_scatter | solution.py:42
  320.3 17.8 %all-gather.16.cloned.1.call-done = bf16[4096,128]{0,1:T(8,128)(2,1)} async-done(((bf16[1024,128]{0,1:T(8,128)(2,1)}), bf16[4096,128]{0,1:T(8,128)(2,1)}) %all-gather.16.cloned.1.call-update) | async-done | bytes 1048592 | tf_op jit(solution)/shard_map/all_gather | solution.py:35
  348.6 18.3 %fusion.75 = bf16[4096,128]{0,1:T(8,128)(2,1)} fusion(bf16[1,4096,2560]{2,1,0:T(8,128)(2,1)} %param.17, bf16[1,4096,2560]{2,1,0:T(8,128)(2,1)} %param.16, f32[2560,128]{0,1:T(8,128)S(1)} %fusion.99, bf16[4096,128]{0,1:T(8,128)(2,1)S(1)} %copy-done.2, f32[4096]{0:T(1024)S(1)} %bitcast.301, f32[128]{0:T(128)S(1)} %add_rsqrt_fusion.5), kind=kOutput, calls=%fused_computation.56 | convolution fusion | flops 5373100032 | bytes 45367808 | tf_op jit(solution)/shard_map/dot_general | solution.py:43
  366.9 24.9 %reduce-scatter.12.cloned.1.call-done = bf16[1024,128]{0,1:T(8,128)(2,1)} async-done(((bf16[4096,128]{0,1:T(8,128)(2,1)}), bf16[1024,128]{0,1:T(8,128)(2,1)}) %reduce-scatter.12.cloned.1.call-update) | async-done | bytes 262160 | tf_op jit(solution)/shard_map/reduce_scatter | solution.py:42
  402.7 17.6 %all-gather.18.cloned.1.call-done = bf16[4096,128]{0,1:T(8,128)(2,1)} async-done(((bf16[1024,128]{0,1:T(8,128)(2,1)}), bf16[4096,128]{0,1:T(8,128)(2,1)}) %all-gather.18.cloned.1.call-update) | async-done | bytes 1048592 | tf_op jit(solution)/shard_map/all_gather | solution.py:35
  421.8 8.9 %fusion.105 = f32[2560,128]{0,1:T(8,128)S(1)} fusion(bf16[1,4096,2560]{2,1,0:T(8,128)(2,1)} %param.15, bf16[4096,128]{0,1:T(8,128)(2,1)} %all-gather.18.cloned.1.call-done, f32[4096]{0:T(1024)S(1)} %bitcast.302, f32[128]{0:T(128)S(1)} %add_rsqrt_fusion.4), kind=kOutput, calls=%fused_computation.66 | convolution fusion | flops 2686255104 | bytes 23347712 | tf_op jit(solution)/shard_map/dot_general | solution.py:23
  430.8 18.3 %fusion.72 = bf16[4096,128]{0,1:T(8,128)(2,1)} fusion(bf16[1,4096,2560]{2,1,0:T(8,128)(2,1)} %param.17, bf16[1,4096,2560]{2,1,0:T(8,128)(2,1)} %param.16, f32[2560,128]{0,1:T(8,128)S(1)} %fusion.105, bf16[4096,128]{0,1:T(8,128)(2,1)S(1)} %copy-done.3, f32[4096]{0:T(1024)S(1)} %bitcast.303, f32[128]{0:T(128)S(1)} %add_rsqrt_fusion.4), kind=kOutput, calls=%fused_computation.55 | convolution fusion | flops 5373100032 | bytes 45367808 | tf_op jit(solution)/shard_map/dot_general | solution.py:43
  449.1 24.9 %reduce-scatter.14.cloned.1.call-done = bf16[1024,128]{0,1:T(8,128)(2,1)} async-done(((bf16[4096,128]{0,1:T(8,128)(2,1)}), bf16[1024,128]{0,1:T(8,128)(2,1)}) %reduce-scatter.14.cloned.1.call-update) | async-done | bytes 262160 | tf_op jit(solution)/shard_map/reduce_scatter | solution.py:42
  484.6 17.8 %all-gather.20.cloned.1.call-done = bf16[4096,128]{0,1:T(8,128)(2,1)} async-done(((bf16[1024,128]{0,1:T(8,128)(2,1)}), bf16[4096,128]{0,1:T(8,128)(2,1)}) %all-gather.20.cloned.1.call-update) | async-done | bytes 1048592 | tf_op jit(solution)/shard_map/all_gather | solution.py:35
  504.0 8.9 %fusion.111 = f32[2560,128]{0,1:T(8,128)S(1)} fusion(bf16[1,4096,2560]{2,1,0:T(8,128)(2,1)} %param.15, bf16[4096,128]{0,1:T(8,128)(2,1)} %all-gather.20.cloned.1.call-done, f32[4096]{0:T(1024)S(1)} %bitcast.304, f32[128]{0:T(128)S(1)} %add_rsqrt_fusion.3), kind=kOutput, calls=%fused_computation.68 | convolution fusion | flops 2686255104 | bytes 23347712 | tf_op jit(solution)/shard_map/dot_general | solution.py:23
  512.9 18.3 %fusion.69 = bf16[4096,128]{0,1:T(8,128)(2,1)} fusion(bf16[1,4096,2560]{2,1,0:T(8,128)(2,1)} %param.17, bf16[1,4096,2560]{2,1,0:T(8,128)(2,1)} %param.16, f32[2560,128]{0,1:T(8,128)S(1)} %fusion.111, bf16[4096,128]{0,1:T(8,128)(2,1)S(1)} %copy-done.4, f32[4096]{0:T(1024)S(1)} %bitcast.305, f32[128]{0:T(128)S(1)} %add_rsqrt_fusion.3), kind=kOutput, calls=%fused_computation.54 | convolution fusion | flops 5373100032 | bytes 45367808 | tf_op jit(solution)/shard_map/dot_general | solution.py:43
  531.3 24.9 %reduce-scatter.16.cloned.1.call-done = bf16[1024,128]{0,1:T(8,128)(2,1)} async-done(((bf16[4096,128]{0,1:T(8,128)(2,1)}), bf16[1024,128]{0,1:T(8,128)(2,1)}) %reduce-scatter.16.cloned.1.call-update) | async-done | bytes 262160 | tf_op jit(solution)/shard_map/reduce_scatter | solution.py:42
  567.0 17.6 %all-gather.22.cloned.1.call-done = bf16[4096,128]{0,1:T(8,128)(2,1)} async-done(((bf16[1024,128]{0,1:T(8,128)(2,1)}), bf16[4096,128]{0,1:T(8,128)(2,1)}) %all-gather.22.cloned.1.call-update) | async-done | bytes 1048592 | tf_op jit(solution)/shard_map/all_gather | solution.py:35
  586.1 8.9 %fusion.117 = f32[2560,128]{0,1:T(8,128)S(1)} fusion(bf16[1,4096,2560]{2,1,0:T(8,128)(2,1)} %param.15, bf16[4096,128]{0,1:T(8,128)(2,1)} %all-gather.22.cloned.1.call-done, f32[4096]{0:T(1024)S(1)} %bitcast.306, f32[128]{0:T(128)S(1)} %add_rsqrt_fusion.2), kind=kOutput, calls=%fused_computation.70 | convolution fusion | flops 2686255104 | bytes 23347712 | tf_op jit(solution)/shard_map/dot_general | solution.py:23
  595.0 18.3 %fusion.66 = bf16[4096,128]{0,1:T(8,128)(2,1)} fusion(bf16[1,4096,2560]{2,1,0:T(8,128)(2,1)} %param.17, bf16[1,4096,2560]{2,1,0:T(8,128)(2,1)} %param.16, f32[2560,128]{0,1:T(8,128)S(1)} %fusion.117, bf16[4096,128]{0,1:T(8,128)(2,1)S(1)} %copy-done.5, f32[4096]{0:T(1024)S(1)} %bitcast.307, f32[128]{0:T(128)S(1)} %add_rsqrt_fusion.2), kind=kOutput, calls=%fused_computation.53 | convolution fusion | flops 5373100032 | bytes 45367808 | tf_op jit(solution)/shard_map/dot_general | solution.py:43
  613.4 24.9 %reduce-scatter.18.cloned.1.call-done = bf16[1024,128]{0,1:T(8,128)(2,1)} async-done(((bf16[4096,128]{0,1:T(8,128)(2,1)}), bf16[1024,128]{0,1:T(8,128)(2,1)}) %reduce-scatter.18.cloned.1.call-update) | async-done | bytes 262160 | tf_op jit(solution)/shard_map/reduce_scatter | solution.py:42
  648.9 17.8 %all-gather.24.cloned.1.call-done = bf16[4096,128]{0,1:T(8,128)(2,1)} async-done(((bf16[1024,128]{0,1:T(8,128)(2,1)}), bf16[4096,128]{0,1:T(8,128)(2,1)}) %all-gather.24.cloned.1.call-update) | async-done | bytes 1048592 | tf_op jit(solution)/shard_map/all_gather | solution.py:35
  668.2 8.9 %fusion.123 = f32[2560,128]{0,1:T(8,128)S(1)} fusion(bf16[1,4096,2560]{2,1,0:T(8,128)(2,1)} %param.15, bf16[4096,128]{0,1:T(8,128)(2,1)} %all-gather.24.cloned.1.call-done, f32[4096]{0:T(1024)S(1)} %bitcast.308, f32[128]{0:T(128)S(1)} %add_rsqrt_fusion.1), kind=kOutput, calls=%fused_computation.72 | convolution fusion | flops 2686255104 | bytes 23347712 | tf_op jit(solution)/shard_map/dot_general | solution.py:23
  677.2 18.3 %fusion.63 = bf16[4096,128]{0,1:T(8,128)(2,1)} fusion(bf16[1,4096,2560]{2,1,0:T(8,128)(2,1)} %param.17, bf16[1,4096,2560]{2,1,0:T(8,128)(2,1)} %param.16, f32[2560,128]{0,1:T(8,128)S(1)} %fusion.123, bf16[4096,128]{0,1:T(8,128)(2,1)S(1)} %copy-done.6, f32[4096]{0:T(1024)S(1)} %bitcast.309, f32[128]{0:T(128)S(1)} %add_rsqrt_fusion.1), kind=kOutput, calls=%fused_computation.52 | convolution fusion | flops 5373100032 | bytes 45367808 | tf_op jit(solution)/shard_map/dot_general | solution.py:43
  696.7 23.8 %reduce-scatter.20.cloned.1.call-done = bf16[1024,128]{0,1:T(8,128)(2,1)} async-done(((bf16[4096,128]{0,1:T(8,128)(2,1)}), bf16[1024,128]{0,1:T(8,128)(2,1)}) %reduce-scatter.20.cloned.1.call-update) | async-done | bytes 262160 | tf_op jit(solution)/shard_map/reduce_scatter | solution.py:42
  721.8 10.1 %all-gather = f32[8192,16]{0,1:T(8,128)S(1)} all-gather(f32[1024,16]{0,1:T(8,128)S(1)} %broadcast_multiply_fusion), channel_id=2, replica_groups=mesh['dp'=2,'section'=4,'mp'=4] {'dp','mp'}, dimensions={0}, use_global_device_ids=true | all-gather | bytes 589824 | tf_op jit(solution)/shard_map/all_gather | solution.py:96
  738.2 10.5 %psum.14 = f32[32,32]{1,0:T(8,128)S(1)} all-reduce(f32[32,32]{1,0:T(8,128)S(1)} %fusion.308), channel_id=1, replica_groups=mesh['dp'=2,'section'=4,'mp'=4] {'mp'}, use_global_device_ids=true, to_apply=%region_17.18 | all-reduce | flops 1024 | bytes 8192 | tf_op jit(solution)/shard_map/psum | solution.py:115
  748.8 18.7 %psum.15 = f32[32,32]{1,0:T(8,128)S(1)} all-reduce(f32[32,32]{1,0:T(8,128)S(1)} %broadcast_select_fusion.4), channel_id=1, replica_groups=mesh['dp'=2,'section'=4,'mp'=4] {'section'}, use_global_device_ids=true, to_apply=%region_18.19 | all-reduce | flops 1024 | bytes 8192 | tf_op jit(solution)/shard_map/psum | solution.py:19
  (152 shorter events, 111.5 us)
Async XLA Ops:
  6.5 147.2 %all-gather.10.cloned.1.call-start = ((), (), s32[]{:S(2)}) async-start(), calls=%async_computation.7 | async-start | bytes 5242880 | tf_op jit(solution)/shard_map/all_gather | solution.py:71
  70.2 103.5 %all-gather.12.cloned.1.call-start = ((), (), s32[]{:S(2)}) async-start(), calls=%async_computation.8 | async-start | bytes 1310720 | tf_op jit(solution)/shard_map/all_gather | solution.py:35
  157.3 18.0 %copy-start.7 = (f32[1,4096]{1,0:T(1,128)S(1)}, f32[1,4096]{1,0:T(1,128)}, u32[]{:S(2)}) copy-start(f32[1,4096]{1,0:T(1,128)} %param.14) | copy-start | bytes 49156
  158.4 69.1 %reduce-scatter.8.cloned.1.call-start = ((), (), s32[]{:S(2)}) async-start(), calls=%async_computation.9 | async-start | bytes 1310720 | tf_op jit(solution)/shard_map/reduce_scatter | solution.py:42
  202.5 53.4 %all-gather.14.cloned.1.call-start = ((), (), s32[]{:S(2)}) async-start(), calls=%async_computation.10 | async-start | bytes 1310720 | tf_op jit(solution)/shard_map/all_gather | solution.py:35
  228.5 8.8 %collective-permute-start = (bf16[1024,128]{0,1:T(8,128)(2,1)S(1)}, bf16[1024,128]{0,1:T(8,128)(2,1)S(1)}, u32[]{:S(2)}, u32[]{:S(2)}) collective-permute-start(bf16[1024,128]{0,1:T(8,128)(2,1)S(1)} %add_convert_fusion.6), channel_id=1, source_target_pairs={{0,4},{4,8},{8,12},{1,5},{5,9},{9,13},{2,6},{6,10},{10,14},{3,7},{... | collective-permute-start | bytes 786440 | tf_op jit(solution)/shard_map/ppermute | solution.py:14
  238.1 71.6 %reduce-scatter.10.cloned.1.call-start = ((), (), s32[]{:S(2)}) async-start(), calls=%async_computation.11 | async-start | bytes 1310720 | tf_op jit(solution)/shard_map/reduce_scatter | solution.py:42
  266.4 43.3 %copy-start.9 = (bf16[1024,128]{0,1:T(8,128)(2,1)S(1)}, bf16[1024,128]{0,1:T(8,128)(2,1)}, u32[]{:S(2)}) copy-start(bf16[1024,128]{0,1:T(8,128)(2,1)} %broadcast_select_fusion.2) | copy-start | bytes 786436
  284.7 53.4 %all-gather.16.cloned.1.call-start = ((), (), s32[]{:S(2)}) async-start(), calls=%async_computation.12 | async-start | bytes 1310720 | tf_op jit(solution)/shard_map/all_gather | solution.py:35
  310.7 8.8 %collective-permute-start.1 = (bf16[1024,128]{0,1:T(8,128)(2,1)S(1)}, bf16[1024,128]{0,1:T(8,128)(2,1)S(1)}, u32[]{:S(2)}, u32[]{:S(2)}) collective-permute-start(bf16[1024,128]{0,1:T(8,128)(2,1)S(1)} %add_convert_fusion.5), channel_id=1, source_target_pairs={{0,4},{4,8},{8,12},{1,5},{5,9},{9,13},{2,6},{6,10},{10,14},{3,7},{... | collective-permute-start | bytes 786440 | tf_op jit(solution)/shard_map/ppermute | solution.py:14
  320.2 71.6 %reduce-scatter.12.cloned.1.call-start = ((), (), s32[]{:S(2)}) async-start(), calls=%async_computation.13 | async-start | bytes 1310720 | tf_op jit(solution)/shard_map/reduce_scatter | solution.py:42
  348.6 43.3 %copy-start.10 = (bf16[1024,128]{0,1:T(8,128)(2,1)S(1)}, bf16[1024,128]{0,1:T(8,128)(2,1)}, u32[]{:S(2)}) copy-start(bf16[1024,128]{0,1:T(8,128)(2,1)} %broadcast_select_fusion.1) | copy-start | bytes 786436
  366.9 53.4 %all-gather.18.cloned.1.call-start = ((), (), s32[]{:S(2)}) async-start(), calls=%async_computation.14 | async-start | bytes 1310720 | tf_op jit(solution)/shard_map/all_gather | solution.py:35
  392.9 8.8 %collective-permute-start.2 = (bf16[1024,128]{0,1:T(8,128)(2,1)S(1)}, bf16[1024,128]{0,1:T(8,128)(2,1)S(1)}, u32[]{:S(2)}, u32[]{:S(2)}) collective-permute-start(bf16[1024,128]{0,1:T(8,128)(2,1)S(1)} %add_convert_fusion.4), channel_id=1, source_target_pairs={{0,4},{4,8},{8,12},{1,5},{5,9},{9,13},{2,6},{6,10},{10,14},{3,7},{... | collective-permute-start | bytes 786440 | tf_op jit(solution)/shard_map/ppermute | solution.py:14
  402.4 71.6 %reduce-scatter.14.cloned.1.call-start = ((), (), s32[]{:S(2)}) async-start(), calls=%async_computation.15 | async-start | bytes 1310720 | tf_op jit(solution)/shard_map/reduce_scatter | solution.py:42
  421.8 8.9 %copy-start.3 = (bf16[4096,128]{0,1:T(8,128)(2,1)S(1)}, bf16[4096,128]{0,1:T(8,128)(2,1)}, u32[]{:S(2)}) copy-start(bf16[4096,128]{0,1:T(8,128)(2,1)} %all-gather.18.cloned.1.call-done) | copy-start | bytes 3145732
  430.8 43.3 %copy-start.8 = (bf16[1024,128]{0,1:T(8,128)(2,1)S(1)}, bf16[1024,128]{0,1:T(8,128)(2,1)}, u32[]{:S(2)}) copy-start(bf16[1024,128]{0,1:T(8,128)(2,1)} %broadcast_select_fusion) | copy-start | bytes 786436
  449.1 53.4 %all-gather.20.cloned.1.call-start = ((), (), s32[]{:S(2)}) async-start(), calls=%async_computation.16 | async-start | bytes 1310720 | tf_op jit(solution)/shard_map/all_gather | solution.py:35
  475.1 8.8 %collective-permute-start.3 = (bf16[1024,128]{0,1:T(8,128)(2,1)S(1)}, bf16[1024,128]{0,1:T(8,128)(2,1)S(1)}, u32[]{:S(2)}, u32[]{:S(2)}) collective-permute-start(bf16[1024,128]{0,1:T(8,128)(2,1)S(1)} %add_convert_fusion.3), channel_id=1, source_target_pairs={{0,4},{4,8},{8,12},{1,5},{5,9},{9,13},{2,6},{6,10},{10,14},{3,7},{... | collective-permute-start | bytes 786440 | tf_op jit(solution)/shard_map/ppermute | solution.py:14
  484.6 71.6 %reduce-scatter.16.cloned.1.call-start = ((), (), s32[]{:S(2)}) async-start(), calls=%async_computation.17 | async-start | bytes 1310720 | tf_op jit(solution)/shard_map/reduce_scatter | solution.py:42
  512.9 43.3 %copy-start.14 = (bf16[1024,128]{0,1:T(8,128)(2,1)S(1)}, bf16[1024,128]{0,1:T(8,128)(2,1)}, u32[]{:S(2)}) copy-start(bf16[1024,128]{0,1:T(8,128)(2,1)} %copy-done.13) | copy-start | bytes 786436
  531.2 53.3 %all-gather.22.cloned.1.call-start = ((), (), s32[]{:S(2)}) async-start(), calls=%async_computation.18 | async-start | bytes 1310720 | tf_op jit(solution)/shard_map/all_gather | solution.py:35
  557.2 8.8 %collective-permute-start.4 = (bf16[1024,128]{0,1:T(8,128)(2,1)S(1)}, bf16[1024,128]{0,1:T(8,128)(2,1)S(1)}, u32[]{:S(2)}, u32[]{:S(2)}) collective-permute-start(bf16[1024,128]{0,1:T(8,128)(2,1)S(1)} %add_convert_fusion.2), channel_id=1, source_target_pairs={{0,4},{4,8},{8,12},{1,5},{5,9},{9,13},{2,6},{6,10},{10,14},{3,7},{... | collective-permute-start | bytes 786440 | tf_op jit(solution)/shard_map/ppermute | solution.py:14
  566.7 71.6 %reduce-scatter.18.cloned.1.call-start = ((), (), s32[]{:S(2)}) async-start(), calls=%async_computation.19 | async-start | bytes 1310720 | tf_op jit(solution)/shard_map/reduce_scatter | solution.py:42
  595.0 43.3 %copy-start.16 = (bf16[1024,128]{0,1:T(8,128)(2,1)S(1)}, bf16[1024,128]{0,1:T(8,128)(2,1)}, u32[]{:S(2)}) copy-start(bf16[1024,128]{0,1:T(8,128)(2,1)} %copy-done.15) | copy-start | bytes 786436
  613.4 53.3 %all-gather.24.cloned.1.call-start = ((), (), s32[]{:S(2)}) async-start(), calls=%async_computation.20 | async-start | bytes 1310720 | tf_op jit(solution)/shard_map/all_gather | solution.py:35
  639.3 8.8 %collective-permute-start.5 = (bf16[1024,128]{0,1:T(8,128)(2,1)S(1)}, bf16[1024,128]{0,1:T(8,128)(2,1)S(1)}, u32[]{:S(2)}, u32[]{:S(2)}) collective-permute-start(bf16[1024,128]{0,1:T(8,128)(2,1)S(1)} %add_convert_fusion.1), channel_id=1, source_target_pairs={{0,4},{4,8},{8,12},{1,5},{5,9},{9,13},{2,6},{6,10},{10,14},{3,7},{... | collective-permute-start | bytes 786440 | tf_op jit(solution)/shard_map/ppermute | solution.py:14
  648.9 71.6 %reduce-scatter.20.cloned.1.call-start = ((), (), s32[]{:S(2)}) async-start(), calls=%async_computation.21 | async-start | bytes 1310720 | tf_op jit(solution)/shard_map/reduce_scatter | solution.py:42
  677.2 18.4 %copy-start.18 = (s32[32]{0:T(128)S(1)}, s32[32]{0:T(128)}, u32[]{:S(2)}) copy-start(s32[32]{0:T(128)} %param.11) | copy-start | bytes 388
  677.2 18.5 %copy-start.19 = (s32[4]{0:T(128)S(1)}, s32[4]{0:T(128)}, u32[]{:S(2)}) copy-start(s32[4]{0:T(128)} %param.12) | copy-start | bytes 52
  677.2 43.3 %copy-start.12 = (bf16[1024,128]{0,1:T(8,128)(2,1)S(1)}, bf16[1024,128]{0,1:T(8,128)(2,1)}, u32[]{:S(2)}) copy-start(bf16[1024,128]{0,1:T(8,128)(2,1)} %copy-done.11) | copy-start | bytes 786436
  721.8 11.2 %copy-start.17 = (f32[4096]{0:T(1024)S(1)}, f32[4096]{0:T(1024)}, u32[]{:S(2)}) copy-start(f32[4096]{0:T(1024)} %param.18) | copy-start | bytes 49156
  (9 other events, 55.8 us)
Sparse Core Ops, SparseCore 0:
  70.3 83.4 all-gather.9
  158.5 15.1 all-gather.11
  202.6 24.8 reduce-scatter.7
  238.2 17.6 all-gather.13
  284.8 24.7 reduce-scatter.9
  320.4 17.6 all-gather.15
  367.0 24.7 reduce-scatter.11
  402.6 17.6 all-gather.17
  449.2 24.8 reduce-scatter.13
  484.7 17.6 all-gather.19
  531.4 24.7 reduce-scatter.15
  566.8 17.7 all-gather.21
  613.5 24.7 reduce-scatter.17
  649.0 17.6 all-gather.23
  695.7 24.7 reduce-scatter.19
